TPU v7x, 256 devices: a whole 4x4x8 slice. The times are simulated.
256 devices in a mesh: tower: 4 (over x_lo, core), seq: 64 (over x_hi, z, y).
Axes of the slice: x: 4 (x_hi: 2, x_lo: 2; x = x_hi * 2 + x_lo), y: 4, z: 8, core: 2. Of those that a mesh axis runs over, the one named last changes fastest.
Arguments:
- queries: bfloat16 [4, 8192, 3072], P('tower', 'seq'), may hold values from -100 to 100
- keys: bfloat16 [4, 8192, 3072], P('tower', 'seq'), may hold values from -4 to 4
- values: bfloat16 [4, 8192, 3072], P('tower', 'seq'), may hold values from -6 to 6
- alignment: int32 [64, 2], replicated, may hold values from 0 to 192, as said below
- cross_gate: float32 [2, 24], replicated, may hold values from 0.5 to 2
Outputs:
- cross_out: bfloat16 [4, 8192, 3072], P('tower', 'seq')
Inputs may be any that keep to these rules, and one draw needn't show every extreme that they name: `alignment`: lo[a] is max(3a - 1, 0) or max(3a, 0); hi[a] is min(3a + 3, 192) or min(3a + 4, 192).
All inputs are finite; a program needn't handle non-finite values.
Results may differ from a plain program's by a relative error of at most 0.0044.
Values may be sent and summed in bfloat16 or wider, within the bound.
A program may use at most 128 MiB of HBM per device.

v0:
```python
import jax
import jax.numpy as jnp
from jax import lax
from jax.sharding import PartitionSpec as P

HEADS = 24
HEAD_DIM = 128
BLOCK = 128


def from_behind(block, axis, distance):
    devices = range(lax.axis_size(axis))
    route = [(i - distance, i) for i in devices if i - distance in devices]
    return lax.ppermute(block, axis, route)


def attend(query_block, key_rows, value_rows, valid, gain):
    count_q = query_block.shape[0]
    count_k = key_rows.shape[0]
    q_heads = query_block.reshape(count_q, HEADS, HEAD_DIM)
    k_heads = key_rows.reshape(count_k, HEADS, HEAD_DIM)
    v_heads = value_rows.reshape(count_k, HEADS, HEAD_DIM)
    scores = jnp.einsum(
        "qhd,khd->hqk", q_heads, k_heads, preferred_element_type=jnp.float32
    ) * HEAD_DIM ** (-0.5)
    scores = jnp.where(valid[None, None, :], scores, -jnp.inf)
    top = jnp.max(scores, axis=2, keepdims=True)
    weights = jnp.exp(scores - top)
    total = jnp.sum(weights, axis=2)
    rounded = weights.astype(jnp.bfloat16)
    mixed = jnp.einsum("hqk,khd->qhd", rounded, v_heads, preferred_element_type=jnp.float32)
    mixed = mixed / jnp.transpose(total)[:, :, None] * gain[None, :, None]
    return mixed.reshape(count_q, HEADS * HEAD_DIM)


def local(queries, keys, values, alignment, cross_gate):
    rows = queries.shape[1]
    per_dev = rows // BLOCK
    seq_count = lax.axis_size("seq")
    column = lax.axis_index("seq")
    section = lax.axis_index("tower")
    lows = alignment[:, 0]
    highs = alignment[:, 1]
    video_total = 3 * per_dev * seq_count
    audio_total = per_dev * seq_count
    local_queries = queries[0]

    def video_path(audio_keys, audio_values):

        def video_step(block):
            index = per_dev * (3 * column + section) + block
            first = index // 3 - 1
            near = first + jnp.arange(3, dtype=jnp.int32)
            safe = jnp.clip(near, 0, audio_total - 1)
            linked = (
                (near >= 0)
                & (near < audio_total)
                & (jnp.take(lows, safe) <= index)
                & (index < jnp.take(highs, safe))
            )
            return attend(
                local_queries, audio_keys, audio_values, jnp.repeat(linked, BLOCK), cross_gate[0]
            )

        return lax.map(video_step, jnp.arange(per_dev, dtype=jnp.int32))

    key_all, value_all = (
        lax.all_gather(keys, "tower", axis=0, tiled=True),
        lax.all_gather(values, "tower", axis=0, tiled=True),
    )
    lower_pack = jnp.stack(
        [
            jnp.stack([key_all[2, rows - BLOCK :], key_all[3, rows - BLOCK :]]),
            jnp.stack([value_all[2, rows - BLOCK :], value_all[3, rows - BLOCK :]]),
        ]
    )
    upper_pack = jnp.stack(
        [
            jnp.stack([key_all[0, :BLOCK], key_all[3, :BLOCK]]),
            jnp.stack([value_all[0, :BLOCK], value_all[3, :BLOCK]]),
        ]
    )
    lower = from_behind(lower_pack, "seq", 1)
    upper = from_behind(upper_pack, "seq", -1)
    lower_video, lower_audio = (lower[:, 0], lower[:, 1])
    upper_video, upper_audio = (upper[:, 0], upper[:, 1])
    video_keys = jnp.concatenate(
        [lower_video[0], key_all[0], key_all[1], key_all[2], upper_video[0]], axis=0
    )
    video_values = jnp.concatenate(
        [lower_video[1], value_all[0], value_all[1], value_all[2], upper_video[1]], axis=0
    )
    audio_keys = jnp.concatenate([lower_audio[0], key_all[3], upper_audio[0]], axis=0)
    audio_values = jnp.concatenate([lower_audio[1], value_all[3], upper_audio[1]], axis=0)

    def audio_path(unused):

        def audio_step(block):
            index = per_dev * column + block
            first = 3 * index - 1
            near = first + jnp.arange(5, dtype=jnp.int32)
            linked = (
                (near >= 0)
                & (near < video_total)
                & (jnp.take(lows, index) <= near)
                & (near < jnp.take(highs, index))
            )
            return attend(
                local_queries, video_keys, video_values, jnp.repeat(linked, BLOCK), cross_gate[1]
            )

        return lax.map(audio_step, jnp.arange(per_dev, dtype=jnp.int32))

    mixed = lax.cond(
        section == 3, audio_path, lambda unused: video_path(audio_keys, audio_values), 0
    )
    return mixed.astype(jnp.bfloat16)


def solution(mesh):
    placed = (P("tower", "seq", None), P("tower", "seq", None), P("tower", "seq", None), P(), P())
    return jax.shard_map(
        local, mesh=mesh, in_specs=placed, out_specs=P("tower", "seq", None), check_vma=False
    )
```

profile of v0, /device:TPU:7, one launch (start us, length us, event | category | flops | bytes accessed | tf_op | source)
XLA Modules:
  0.0 233.7 jit_solution(7783236076697758818)
XLA Ops:
  8.0 44.2 %all-gather.5.cloned.1.call-done = bf16[4,128,3072]{2,1,0:T(8,128)(2,1)} async-done(((bf16[1,128,3072]{2,1,0:T(8,128)(2,1)}), bf16[4,128,3072]{2,1,0:T(8,128)(2,1)}) %all-gather.5.cloned.1.call-update) | async-done | bytes 3145744 | tf_op jit(solution)/shard_map/all_gather | solution.py:69
  52.2 2.5 %slice_bitcast_fusion.18 = (bf16[128,3072]{1,0:T(8,128)(2,1)}, bf16[1,128,3072]{2,1,0:T(8,128)(2,1)S(1)}, bf16[1,128,3072]{2,1,0:T(8,128)(2,1)S(1)}) fusion(bf16[4,128,3072]{2,1,0:T(8,128)(2,1)} %all-gather.5.cloned.1.call-done), kind=kLoop, calls=%fused_computation.80 | loop fusion | bytes 3932160 | tf_op jit(solution)/shard_map/squeeze | solution.py:94
  54.8 40.5 %all-gather.3.cloned.1.call-done = bf16[4,128,3072]{2,1,0:T(8,128)(2,1)} async-done(((bf16[1,128,3072]{2,1,0:T(8,128)(2,1)}), bf16[4,128,3072]{2,1,0:T(8,128)(2,1)}) %all-gather.3.cloned.1.call-update) | async-done | bytes 3145744 | tf_op jit(solution)/shard_map/all_gather | solution.py:68
  95.3 2.5 %slice_bitcast_fusion.19 = (bf16[128,3072]{1,0:T(8,128)(2,1)}, bf16[1,128,3072]{2,1,0:T(8,128)(2,1)S(1)}, bf16[1,128,3072]{2,1,0:T(8,128)(2,1)S(1)}) fusion(bf16[4,128,3072]{2,1,0:T(8,128)(2,1)} %all-gather.3.cloned.1.call-done), kind=kLoop, calls=%fused_computation.81 | loop fusion | bytes 3932160 | tf_op jit(solution)/shard_map/squeeze | solution.py:93
  98.1 1.9 pad_maximum_fusion.1
  100.0 8.0 %collective-permute-start.1 = (bf16[2,2,128,3072]{3,2,1,0:T(8,128)(2,1)}, bf16[2,2,128,3072]{3,2,1,0:T(8,128)(2,1)}, u32[]{:S(2)}, u32[]{:S(2)}) collective-permute-start(bf16[2,2,128,3072]{3,2,1,0:T(8,128)(2,1)} %pad_maximum_fusion.1), channel_id=1, source_target_pairs={{1,0},{2,1},{3,2},{4,3},{5,4},{6,5},{7,6},{8,7},{9,8},{10,9},{11,1... | collective-permute-start | bytes 9437192 | tf_op jit(solution)/shard_map/ppermute | solution.py:14
  108.2 2.0 pad_maximum_fusion
  110.1 1.9 collective-permute-start
  112.1 63.8 %collective-permute-done.1 = bf16[2,2,128,3072]{3,2,1,0:T(8,128)(2,1)} collective-permute-done((bf16[2,2,128,3072]{3,2,1,0:T(8,128)(2,1)}, bf16[2,2,128,3072]{3,2,1,0:T(8,128)(2,1)}, u32[]{:S(2)}, u32[]{:S(2)}) %collective-permute-start.1) | collective-permute-done | bytes 3145760 | tf_op jit(solution)/shard_map/ppermute | solution.py:14
  176.0 1.5 slice_bitcast_fusion.12
  177.4 10.3 %collective-permute-done = bf16[2,2,128,3072]{3,2,1,0:T(8,128)(2,1)} collective-permute-done((bf16[2,2,128,3072]{3,2,1,0:T(8,128)(2,1)}, bf16[2,2,128,3072]{3,2,1,0:T(8,128)(2,1)}, u32[]{:S(2)}, u32[]{:S(2)}) %collective-permute-start) | collective-permute-done | bytes 3145760 | tf_op jit(solution)/shard_map/ppermute | solution.py:14
  187.7 1.5 slice_bitcast_fusion.13
  189.2 1.6 pad_maximum_fusion.3
  190.8 1.6 pad_maximum_fusion.2
  192.4 2.8 %fusion.39 = (bf16[640,3072]{1,0:T(8,128)(2,1)}, bf16[640,3072]{1,0:T(8,128)(2,1)}) fusion(bf16[2,2,128,3072]{3,2,1,0:T(8,128)(2,1)} %collective-permute-done), kind=kLoop, calls=%fused_computation.63 | loop fusion | bytes 3145728
  195.2 1.2 bitcast_dynamic-update-slice_fusion
  200.2 2.6 %fusion.36 = (bf16[640,3072]{1,0:T(8,128)(2,1)}, bf16[640,3072]{1,0:T(8,128)(2,1)}) fusion(bf16[640,3072]{1,0:T(8,128)(2,1)} %fusion.37, bf16[2,2,128,3072]{3,2,1,0:T(8,128)(2,1)} %collective-permute-done.1, bf16[640,3072]{1,0:T(8,128)(2,1)} %fusion.41), kind=kLoop, calls=%fused_computation.57 | loop fusion | bytes 3145728 | tf_op jit(solution)/shard_map/concatenate | solution.py:90
  202.8 22.9 %conditional.6 = (bf16[1,128,3072]{1,2,0:T(8,128)(2,1)S(1)}) conditional(s32[]{:T(128)} %convert_element_type.28, (s32[]{:T(128)}, s32[]{:T(128)}, s32[64]{0:T(128)S(1)}, s32[64]{0:T(128)S(1)}, bf16[1,128,3072]{2,1,0:T(8,128)(2,1)S(1)}, /*index=5*/bf16[384,3072]{1,0:T(8,128)(2,1)}, bf16[384,3072]{1,0:T(8,128)(2,1)S(1)}, ...), branch_computations={%region_0.4_spmd, %region_3.7_spmd} | conditional | flops 1029433408 | bytes 73989080
  205.7 3.8 %fusion = (f32[24,128]{1,0:T(8,128)S(1)}, f32[24,128,640]{2,1,0:T(8,128)S(1)}) fusion(pred[640]{0:T(1024)(128)(4,1)S(1)} %broadcast_bitcast_fusion, bf16[128,24,128]{2,1,0:T(8,128)(2,1)S(1)} %bitcast.114, bf16[640,3072]{1,0:T(8,128)(2,1)} %get-tuple-element.114), kind=kOutput, calls=%fused_computation.4 | convolution fusion | flops 509211648 | bytes 12595840 | tf_op jit(solution)/shard_map/cond/branch_1_fun/while/body/eval_jaxpr/qhd,khd->hqk/dot_general | solution.py:23
  209.5 2.0 fusion.1
  211.5 1.2 copy-done
  212.7 6.2 %copy.29 = bf16[640,3072]{0,1:T(8,128)(2,1)} copy(bf16[640,3072]{1,0:T(8,128)(2,1)} %get-tuple-element.182) | data formatting | bytes 7864320 | tf_op jit(solution)/shard_map
  218.8 6.9 %fusion.12 = bf16[128,24,128]{0,2,1:T(8,128)(2,1)S(1)} fusion(bf16[640,24,128]{0,2,1:T(8,128)(2,1)} %bitcast.111, f32[24,128,640]{2,1,0:T(8,128)} %copy-done, f32[24,128]{1,0:T(8,128)S(1)} %get-tuple-element.184, pred[640]{0:T(1024)(128)(4,1)S(1)} %broadcast_bitcast_fusion, f32[24]{0:T(128)S(1)} %slice_bitcast_fusion, f32[128,24]{0,1:T(8,128)S(1)} %bitcast.120), kind=kOutput, calls=%fused_computation.16 | convolution fusion | flops 512360448 | bytes 12608224 | tf_op jit(solution)/shard_map/cond/branch_1_fun/while/body/eval_jaxpr/hqk,khd->qhd/dot_general | solution.py:31
  225.7 1.2 copy.30
  (37 shorter events, 7.2 us)
Async XLA Ops:
  6.5 45.7 %all-gather.5.cloned.1.call-start = ((), (), s32[]{:S(2)}) async-start(), calls=%async_computation.1 | async-start | bytes 3932160 | tf_op jit(solution)/shard_map/all_gather | solution.py:69
  7.3 88.0 %all-gather.3.cloned.1.call-start = ((), (), s32[]{:S(2)}) async-start(), calls=%async_computation | async-start | bytes 3932160 | tf_op jit(solution)/shard_map/all_gather | solution.py:68
  98.0 9.9 %copy-start.1 = (bf16[4,128,3072]{2,1,0:T(8,128)(2,1)S(1)}, bf16[4,128,3072]{2,1,0:T(8,128)(2,1)}, u32[]{:S(2)}) copy-start(bf16[4,128,3072]{2,1,0:T(8,128)(2,1)} %all-gather.5.cloned.1.call-done) | copy-start | bytes 9437188
  98.0 10.0 %copy-start.2 = (bf16[4,128,3072]{2,1,0:T(8,128)(2,1)S(1)}, bf16[4,128,3072]{2,1,0:T(8,128)(2,1)}, u32[]{:S(2)}) copy-start(bf16[4,128,3072]{2,1,0:T(8,128)(2,1)} %all-gather.3.cloned.1.call-done) | copy-start | bytes 9437188
  100.0 76.0 %collective-permute-start.1 = (bf16[2,2,128,3072]{3,2,1,0:T(8,128)(2,1)}, bf16[2,2,128,3072]{3,2,1,0:T(8,128)(2,1)}, u32[]{:S(2)}, u32[]{:S(2)}) collective-permute-start(bf16[2,2,128,3072]{3,2,1,0:T(8,128)(2,1)} %pad_maximum_fusion.1), channel_id=1, source_target_pairs={{1,0},{2,1},{3,2},{4,3},{5,4},{6,5},{7,6},{8,7},{9,8},{10,9},{11,1... | collective-permute-start | bytes 9437192 | tf_op jit(solution)/shard_map/ppermute | solution.py:14
  108.2 3.9 %copy-start.9 = (s32[64,2]{0,1:T(2,128)S(1)}, s32[64,2]{0,1:T(2,128)}, u32[]{:S(2)}) copy-start(s32[64,2]{0,1:T(2,128)} %param.12) | copy-start | bytes 1540
  110.1 77.6 %collective-permute-start = (bf16[2,2,128,3072]{3,2,1,0:T(8,128)(2,1)}, bf16[2,2,128,3072]{3,2,1,0:T(8,128)(2,1)}, u32[]{:S(2)}, u32[]{:S(2)}) collective-permute-start(bf16[2,2,128,3072]{3,2,1,0:T(8,128)(2,1)} %pad_maximum_fusion), channel_id=1, source_target_pairs={{0,1},{1,2},{2,3},{3,4},{4,5},{5,6},{6,7},{7,8},{8,9},{9,10},{10,1... | collective-permute-start | bytes 9437192 | tf_op jit(solution)/shard_map/ppermute | solution.py:14
  112.1 77.1 %copy-start.7 = (bf16[128,3072]{1,0:T(8,128)(2,1)S(1)}, bf16[128,3072]{1,0:T(8,128)(2,1)}, u32[]{:S(2)}) copy-start(bf16[128,3072]{1,0:T(8,128)(2,1)} %get-tuple-element.194) | copy-start | bytes 2359300
  177.4 13.3 %copy-start.8 = (bf16[128,3072]{1,0:T(8,128)(2,1)S(1)}, bf16[128,3072]{1,0:T(8,128)(2,1)}, u32[]{:S(2)}) copy-start(bf16[128,3072]{1,0:T(8,128)(2,1)} %get-tuple-element.199) | copy-start | bytes 2359300
  190.8 4.4 %copy-start.3 = (bf16[4,128,3072]{2,1,0:T(8,128)(2,1)S(1)}, bf16[4,128,3072]{2,1,0:T(8,128)(2,1)}, u32[]{:S(2)}) copy-start(bf16[4,128,3072]{2,1,0:T(8,128)(2,1)} %all-gather.3.cloned.1.call-done) | copy-start | bytes 9437188
  197.4 5.5 %copy-start.10 = (f32[2,24]{1,0:T(2,128)S(1)}, f32[2,24]{1,0:T(2,128)}, u32[]{:S(2)}) copy-start(f32[2,24]{1,0:T(2,128)} %param.13) | copy-start | bytes 580
  198.3 4.5 %copy-start.4 = (bf16[384,3072]{1,0:T(8,128)(2,1)S(1)}, bf16[384,3072]{1,0:T(8,128)(2,1)}, u32[]{:S(2)}) copy-start(bf16[384,3072]{1,0:T(8,128)(2,1)} %pad_maximum_fusion.3) | copy-start | bytes 7077892
  198.3 4.5 %copy-start.6 = (bf16[1,128,3072]{2,1,0:T(8,128)(2,1)S(1)}, bf16[1,128,3072]{2,1,0:T(8,128)(2,1)}, u32[]{:S(2)}) copy-start(bf16[1,128,3072]{2,1,0:T(8,128)(2,1)} %param.9) | copy-start | bytes 2359300
  209.5 3.1 %copy-start = (f32[24,128,640]{2,1,0:T(8,128)}, f32[24,128,640]{2,1,0:T(8,128)S(1)}, u32[]{:S(2)}) copy-start(f32[24,128,640]{2,1,0:T(8,128)S(1)} %get-tuple-element.185) | copy-start | bytes 23592964 | tf_op jit(solution)/shard_map/conditional.1
Sparse Core Ops, SparseCore 0:
  9.1 43.0 all-gather.4
  54.0 41.2 all-gather.2
where the time goes:
time: 234 us
  waiting for transfers between devices  160 us (68%)
  local copies, waits for them, and re-layouts  28.5 us (12%)
  between operations  13.5 us (6%)
  matrix products  10.7 us (5%)
  starting transfers between devices  9.92 us (4%)
  other arithmetic  9.3 us (4%)
    ppermute x2, waiting for transfers between devices, from_behind(): return lax.ppermute(block, axis, route)  74.1 us
    all_gather x1, waiting for transfers between devices, local(): lax.all_gather(values, 'tower', axis=0, tiled=True)  44.2 us
    all_gather x1, waiting for transfers between devices, local(): lax.all_gather(keys, 'tower', axis=0, tiled=True)  40.5 us
    ppermute x2, starting transfers between devices, from_behind(): return lax.ppermute(block, axis, route)  9.87 us
    unnamed x24, local copies, waits for them, and re-layouts  7.85 us
    another operation x4, local copies, waits for them, and re-layouts  7.48 us
    dot_general x1, matrix products, attend(): jnp.einsum('hqk,khd->qhd', rounded, v_heads, preferred_element_type=jnp.f...  6.88 us
  transfers between devices with their start and end apart: 4, of which 4 were waited for; matrix products, arithmetic and copies ran while one was open for 3% of the time, Pallas kernels for 0%

commit v1 on v0

--- a/solution.py
+++ b/solution.py
@@ -66,7 +66,9 @@
 
     key_all, value_all = (
         lax.all_gather(keys, "tower", axis=0, tiled=True),
-        lax.all_gather(values, "tower", axis=0, tiled=True),
+        jnp.concatenate(
+            lax.all_to_all(jnp.stack([values] * lax.axis_size("tower")), "tower", 0, 0), axis=0
+        ),
     )
     lower_pack = jnp.stack(
         [

time: 234 us -> 215 us (0.919)
  waiting for transfers between devices: 160 us -> 75.8 us
  blocking collectives: 0 us -> 59.1 us
  starting transfers between devices: 9.92 us -> 13.4 us
    all_to_all x0 -> x1, blocking collectives: none -> 59.1 us  [local(): lax.all_to_all(jnp.stack([values] * lax.axis_size('tower')), 'tower', 0, 0)]
    all_gather x1 -> x0, waiting for transfers between devices: 44.2 us -> none  [local(): lax.all_gather(values, 'tower', axis=0, tiled=True)]
    all_gather x1, waiting for transfers between devices: 40.5 us -> 2.05 us  [local(): lax.all_gather(keys, 'tower', axis=0, tiled=True)]
    ppermute x2, starting transfers between devices: 9.87 us -> 13.4 us  [from_behind(): return lax.ppermute(block, axis, route)]
    another operation x4 -> x5, local copies, waits for them, and re-layouts: 7.48 us -> 10.2 us
    unnamed x24 -> x22, local copies, waits for them, and re-layouts: 7.85 us -> 7.76 us
  transfers between devices with their start and end apart: 4 -> 3, of which waited for: 4 -> 3; matrix products, arithmetic and copies ran while one was open for 3% -> 4% of each run, Pallas kernels for 0% -> 0%
where the time goes in v1:
time: 215 us
  waiting for transfers between devices  75.8 us (35%)
  blocking collectives  59.1 us (27%)
  local copies, waits for them, and re-layouts  30.1 us (14%)
  between operations  13.6 us (6%)
  starting transfers between devices  13.4 us (6%)
  matrix products  10.7 us (5%)
  other arithmetic  10.6 us (5%)
    ppermute x2, waiting for transfers between devices, from_behind(): return lax.ppermute(block, axis, route)  73 us
    all_to_all x1, blocking collectives, local(): lax.all_to_all(jnp.stack([values] * lax.axis_size('tower')), 'tower', 0, 0)  59.1 us
    ppermute x2, starting transfers between devices, from_behind(): return lax.ppermute(block, axis, route)  13.4 us
    another operation x4, local copies, waits for them, and re-layouts  8.71 us
    unnamed x22, local copies, waits for them, and re-layouts  7.76 us
    dot_general x1, matrix products, attend(): jnp.einsum('hqk,khd->qhd', rounded, v_heads, preferred_element_type=jnp.f...  6.88 us
  transfers between devices with their start and end apart: 3, of which 3 were waited for; matrix products, arithmetic and copies ran while one was open for 4% of the time, Pallas kernels for 0%

profile of v1, /device:TPU:7, one launch (start us, length us, event | category | flops | bytes accessed | tf_op | source)
XLA Modules:
  0.0 214.5 jit_solution(9601372963733712683)
XLA Ops:
  7.3 1.5 stack.39
  8.8 59.1 %all_to_all.5 = bf16[4,1,128,3072]{3,2,1,0:T(8,128)(2,1)S(1)} all-to-all(bf16[4,1,128,3072]{3,2,1,0:T(8,128)(2,1)S(1)} %stack.39), channel_id=1, replica_groups=mesh['tower'=4,'seq'=64] {'tower'}, dimensions={0} | all-to-all | bytes 6291456 | tf_op jit(solution)/shard_map/all_to_all | solution.py:70
  67.8 1.2 slice_bitcast_fusion.15
  69.0 1.9 fusion.36
  70.9 2.1 all-gather.2.cloned.1.call-done
  73.0 2.7 %slice_bitcast_fusion.20 = (bf16[128,3072]{1,0:T(8,128)(2,1)}, bf16[1,128,3072]{2,1,0:T(8,128)(2,1)S(1)}, bf16[1,128,3072]{2,1,0:T(8,128)(2,1)S(1)}) fusion(bf16[4,128,3072]{2,1,0:T(8,128)(2,1)} %all-gather.2.cloned.1.call-done), kind=kLoop, calls=%fused_computation.85 | loop fusion | bytes 3932160 | tf_op jit(solution)/shard_map/squeeze | solution.py:95
  75.9 2.0 pad_maximum_fusion.1
  77.9 11.5 %collective-permute-start.1 = (bf16[2,2,128,3072]{3,2,1,0:T(8,128)(2,1)}, bf16[2,2,128,3072]{3,2,1,0:T(8,128)(2,1)}, u32[]{:S(2)}, u32[]{:S(2)}) collective-permute-start(bf16[2,2,128,3072]{3,2,1,0:T(8,128)(2,1)} %pad_maximum_fusion.1), channel_id=1, source_target_pairs={{1,0},{2,1},{3,2},{4,3},{5,4},{6,5},{7,6},{8,7},{9,8},{10,9},{11,1... | collective-permute-start | bytes 9437192 | tf_op jit(solution)/shard_map/ppermute | solution.py:14
  89.5 1.9 pad_maximum_fusion
  91.4 1.9 collective-permute-start
  93.4 62.9 %collective-permute-done.1 = bf16[2,2,128,3072]{3,2,1,0:T(8,128)(2,1)} collective-permute-done((bf16[2,2,128,3072]{3,2,1,0:T(8,128)(2,1)}, bf16[2,2,128,3072]{3,2,1,0:T(8,128)(2,1)}, u32[]{:S(2)}, u32[]{:S(2)}) %collective-permute-start.1) | collective-permute-done | bytes 3145760 | tf_op jit(solution)/shard_map/ppermute | solution.py:14
  156.3 1.5 slice_bitcast_fusion.10
  157.7 10.2 %collective-permute-done = bf16[2,2,128,3072]{3,2,1,0:T(8,128)(2,1)} collective-permute-done((bf16[2,2,128,3072]{3,2,1,0:T(8,128)(2,1)}, bf16[2,2,128,3072]{3,2,1,0:T(8,128)(2,1)}, u32[]{:S(2)}, u32[]{:S(2)}) %collective-permute-start) | collective-permute-done | bytes 3145760 | tf_op jit(solution)/shard_map/ppermute | solution.py:14
  167.9 1.5 slice_bitcast_fusion.11
  169.4 2.6 %pad_maximum_fusion.2 = (bf16[384,3072]{1,0:T(8,128)(2,1)}, bf16[384,3072]{1,0:T(8,128)(2,1)}) fusion(bf16[128,3072]{1,0:T(8,128)(2,1)S(1)} %get-tuple-element.199, bf16[128,3072]{1,0:T(8,128)(2,1)S(1)} %copy-done.8, bf16[128,3072]{1,0:T(8,128)(2,1)S(1)} %get-tuple-element.193, bf16[128,3072]{1,0:T(8,128)(2,1)S(1)} %get-tuple-element.198, ...), kind=kLoop, calls=%fused_computation.50 | loop fusion | flops 14155776 | bytes 9437184 | tf_op jit(solution)/shard_map/concatenate | solution.py:95
  172.0 2.7 %fusion.40 = (bf16[640,3072]{1,0:T(8,128)(2,1)}, bf16[640,3072]{1,0:T(8,128)(2,1)}) fusion(bf16[2,2,128,3072]{3,2,1,0:T(8,128)(2,1)} %collective-permute-done), kind=kLoop, calls=%fused_computation.63 | loop fusion | bytes 3145728
  174.7 1.3 bitcast_dynamic-update-slice_fusion.1
  179.7 2.6 %fusion.38 = (bf16[640,3072]{1,0:T(8,128)(2,1)}, bf16[640,3072]{1,0:T(8,128)(2,1)}) fusion(bf16[640,3072]{1,0:T(8,128)(2,1)} %bitcast_dynamic-update-slice_fusion, bf16[2,2,128,3072]{3,2,1,0:T(8,128)(2,1)} %collective-permute-done.1, bf16[640,3072]{1,0:T(8,128)(2,1)} %fusion.42), kind=kLoop, calls=%fused_computation.59 | loop fusion | bytes 3145728 | tf_op jit(solution)/shard_map/concatenate | solution.py:92
  182.4 24.1 %conditional.6 = (bf16[1,128,3072]{1,2,0:T(8,128)(2,1)S(1)}) conditional(s32[]{:T(128)} %convert_element_type.28, (s32[]{:T(128)}, s32[]{:T(128)}, s32[64]{0:T(128)S(1)}, s32[64]{0:T(128)S(1)}, bf16[1,128,3072]{2,1,0:T(8,128)(2,1)}, /*index=5*/bf16[384,3072]{1,0:T(8,128)(2,1)}, bf16[384,3072]{1,0:T(8,128)(2,1)}, f32[2,24]{1,0:T(2,128)S(1)}) %tuple.63, ...), branch_computations={%region_0.4_spmd, %region_3.7_spmd} | conditional | flops 1029433408 | bytes 73989080
  185.1 1.3 copy.32
  186.3 3.8 %fusion = (f32[24,128]{1,0:T(8,128)S(1)}, f32[24,128,640]{2,1,0:T(8,128)S(1)}) fusion(pred[640]{0:T(1024)(128)(4,1)S(1)} %broadcast_bitcast_fusion, bf16[128,24,128]{2,1,0:T(8,128)(2,1)S(1)} %bitcast.119, bf16[640,3072]{1,0:T(8,128)(2,1)} %get-tuple-element.114), kind=kOutput, calls=%fused_computation.4 | convolution fusion | flops 509211648 | bytes 12595840 | tf_op jit(solution)/shard_map/cond/branch_1_fun/while/body/eval_jaxpr/qhd,khd->hqk/dot_general | solution.py:23
  190.2 2.0 fusion.1
  193.2 6.4 %copy.29 = bf16[640,3072]{0,1:T(8,128)(2,1)} copy(bf16[640,3072]{1,0:T(8,128)(2,1)} %get-tuple-element.182) | data formatting | bytes 7864320 | tf_op jit(solution)/shard_map
  199.6 6.9 %fusion.12 = bf16[128,24,128]{0,2,1:T(8,128)(2,1)S(1)} fusion(bf16[640,24,128]{0,2,1:T(8,128)(2,1)} %bitcast.116, f32[24,128,640]{2,1,0:T(8,128)} %copy-done, f32[24,128]{1,0:T(8,128)S(1)} %get-tuple-element.184, pred[640]{0:T(1024)(128)(4,1)S(1)} %broadcast_bitcast_fusion, f32[24]{0:T(128)S(1)} %slice_bitcast_fusion, f32[128,24]{0,1:T(8,128)S(1)} %bitcast.126), kind=kOutput, calls=%fused_computation.16 | convolution fusion | flops 512360448 | bytes 12608224 | tf_op jit(solution)/shard_map/cond/branch_1_fun/while/body/eval_jaxpr/hqk,khd->qhd/dot_general | solution.py:31
  (33 shorter events, 8.4 us)
Async XLA Ops:
  6.5 66.5 %all-gather.2.cloned.1.call-start = ((), (), s32[]{:S(2)}) async-start(), calls=%async_computation.1 | async-start | bytes 3932160 | tf_op jit(solution)/shard_map/all_gather | solution.py:68
  73.0 2.9 %copy-start.5 = (bf16[1,2,128,3072]{3,2,1,0:T(8,128)(2,1)S(1)}, bf16[1,2,128,3072]{3,2,1,0:T(8,128)(2,1)}, u32[]{:S(2)}) copy-start(bf16[1,2,128,3072]{3,2,1,0:T(8,128)(2,1)} %get-tuple-element.204) | copy-start | bytes 4718596
  75.9 13.5 %copy-start.1 = (bf16[4,128,3072]{2,1,0:T(8,128)(2,1)S(1)}, bf16[4,128,3072]{2,1,0:T(8,128)(2,1)}, u32[]{:S(2)}) copy-start(bf16[4,128,3072]{2,1,0:T(8,128)(2,1)} %all-gather.2.cloned.1.call-done) | copy-start | bytes 9437188
  75.9 13.6 %copy-start.4 = (bf16[1,2,128,3072]{3,2,1,0:T(8,128)(2,1)S(1)}, bf16[1,2,128,3072]{3,2,1,0:T(8,128)(2,1)}, u32[]{:S(2)}) copy-start(bf16[1,2,128,3072]{3,2,1,0:T(8,128)(2,1)} %get-tuple-element.203) | copy-start | bytes 4718596
  77.9 78.4 %collective-permute-start.1 = (bf16[2,2,128,3072]{3,2,1,0:T(8,128)(2,1)}, bf16[2,2,128,3072]{3,2,1,0:T(8,128)(2,1)}, u32[]{:S(2)}, u32[]{:S(2)}) collective-permute-start(bf16[2,2,128,3072]{3,2,1,0:T(8,128)(2,1)} %pad_maximum_fusion.1), channel_id=1, source_target_pairs={{1,0},{2,1},{3,2},{4,3},{5,4},{6,5},{7,6},{8,7},{9,8},{10,9},{11,1... | collective-permute-start | bytes 9437192 | tf_op jit(solution)/shard_map/ppermute | solution.py:14
  89.5 3.9 %copy-start.9 = (s32[64,2]{0,1:T(2,128)S(1)}, s32[64,2]{0,1:T(2,128)}, u32[]{:S(2)}) copy-start(s32[64,2]{0,1:T(2,128)} %param.12) | copy-start | bytes 1540
  91.4 76.5 %collective-permute-start = (bf16[2,2,128,3072]{3,2,1,0:T(8,128)(2,1)}, bf16[2,2,128,3072]{3,2,1,0:T(8,128)(2,1)}, u32[]{:S(2)}, u32[]{:S(2)}) collective-permute-start(bf16[2,2,128,3072]{3,2,1,0:T(8,128)(2,1)} %pad_maximum_fusion), channel_id=1, source_target_pairs={{0,1},{1,2},{2,3},{3,4},{4,5},{5,6},{6,7},{7,8},{8,9},{9,10},{10,1... | collective-permute-start | bytes 9437192 | tf_op jit(solution)/shard_map/ppermute | solution.py:14
  93.4 76.0 %copy-start.7 = (bf16[128,3072]{1,0:T(8,128)(2,1)S(1)}, bf16[128,3072]{1,0:T(8,128)(2,1)}, u32[]{:S(2)}) copy-start(bf16[128,3072]{1,0:T(8,128)(2,1)} %get-tuple-element.194) | copy-start | bytes 2359300
  93.4 76.0 %copy-start.8 = (bf16[128,3072]{1,0:T(8,128)(2,1)S(1)}, bf16[128,3072]{1,0:T(8,128)(2,1)}, u32[]{:S(2)}) copy-start(bf16[128,3072]{1,0:T(8,128)(2,1)} %get-tuple-element.200) | copy-start | bytes 2359300
  169.4 5.3 %copy-start.2 = (bf16[4,128,3072]{2,1,0:T(8,128)(2,1)S(1)}, bf16[4,128,3072]{2,1,0:T(8,128)(2,1)}, u32[]{:S(2)}) copy-start(bf16[4,128,3072]{2,1,0:T(8,128)(2,1)} %all-gather.2.cloned.1.call-done) | copy-start | bytes 9437188
  176.9 5.4 %copy-start.10 = (f32[2,24]{1,0:T(2,128)S(1)}, f32[2,24]{1,0:T(2,128)}, u32[]{:S(2)}) copy-start(f32[2,24]{1,0:T(2,128)} %param.13) | copy-start | bytes 580
  190.2 3.1 %copy-start = (f32[24,128,640]{2,1,0:T(8,128)}, f32[24,128,640]{2,1,0:T(8,128)S(1)}, u32[]{:S(2)}) copy-start(f32[24,128,640]{2,1,0:T(8,128)S(1)} %get-tuple-element.185) | copy-start | bytes 23592964 | tf_op jit(solution)/shard_map/conditional.1
Sparse Core Ops, SparseCore 0:
  9.1 63.8 all-gather.1
